TPU v7x, 32 devices: a whole 2x2x4 slice. The times are simulated.
32 devices in a mesh: db: 16 (over z, x, core), mp: 2 (over y).
Axes of the slice: x: 2, y: 2, z: 4, core: 2. Of those that a mesh axis runs over, the one named last changes fastest.
Arguments:
- queries: bfloat16 [32768, 2048], P('db', 'mp'), may hold values from -400 to 400, as said below
- encodings: bfloat16 [512, 128, 896], P(('db', 'mp')), may hold values from -6 to 6
- key_weight: bfloat16 [896, 2048], P('db', 'mp'), may hold values from -0.1875 to 0.1875
- value_weight: bfloat16 [896, 2048], P('db', 'mp'), may hold values from -0.1875 to 0.1875
- nbr_shard: int32 [512, 2], P('db'), may hold values from 0 to 15, all different within a row; in each aligned block of 32 rows (0 to 31, 32 to 63, ...) at most 8 rows name the same one
- nbr_row: int32 [512, 2], P('db'), may hold values from 0 to 31
Outputs:
- cross_out: bfloat16 [32768, 2048], P('db', 'mp')
Inputs may be any that keep to these rules, and one draw needn't show every extreme that they name: `queries`: some query rows may be far larger than the rest. `nbr_shard`: among the spans of one index of db no shard is named by more than 8 spans; the 2 shards of one span differ.
All inputs are finite; a program needn't handle non-finite values.
Results may differ from a plain program's by a relative error of at most 0.025.
Values may be sent and summed in bfloat16 or wider, within the bound.
No kernel may reach another device: no remote copies, remote signals or barrier semaphores. Data moves between devices by JAX's collectives and lax.ppermute only.
A program may use at most 256 MiB of HBM per device.

v0:
```python
import math
import jax
import jax.numpy as jnp
from jax import lax
from jax.sharding import PartitionSpec as P

DH = 128
SPAN = 64
SEQ = 128


def attend(queried, key_block, value_block, head_dim):
    batch_size, length, columns = queried.shape
    head_count = columns // head_dim
    query_heads = queried.reshape(batch_size, length, head_count, head_dim)
    key_heads = key_block.reshape(batch_size, key_block.shape[1], head_count, head_dim)
    value_heads = value_block.reshape(batch_size, value_block.shape[1], head_count, head_dim)
    scores = jnp.einsum(
        "bqhd,bkhd->bhqk", query_heads, key_heads, preferred_element_type=jnp.float32
    ) * (1.0 / math.sqrt(head_dim))
    row_max = jnp.max(scores, axis=-1)
    expscore = jnp.exp(scores - row_max[..., None])
    row_sum = jnp.sum(expscore, axis=-1)
    partial_value = jnp.einsum(
        "bhqk,bkhd->bqhd",
        expscore.astype(jnp.bfloat16),
        value_heads,
        preferred_element_type=jnp.float32,
    )
    return (
        partial_value.reshape(batch_size, length, columns).astype(jnp.bfloat16),
        row_max,
        row_sum,
    )


def local(queries, encodings, key_weight, value_weight, nbr_shard, nbr_row):
    shards = lax.axis_size("db")
    columns = queries.shape[1]
    head_count = columns // DH
    span_count = nbr_shard.shape[0]
    neighbours = nbr_shard.shape[1]
    capacity = max(2, 4 * span_count // shards)
    slots = shards * capacity
    full_keys, full_values = (
        lax.all_gather(key_weight, "db", axis=0, tiled=True),
        lax.all_gather(value_weight, "db", axis=0, tiled=True),
    )
    both_weights = jnp.concatenate([full_keys, full_values], axis=1)
    piece = lax.all_gather(encodings, "mp", axis=0, tiled=True)
    flat = piece.reshape(piece.shape[0] * piece.shape[1], piece.shape[2])
    mixed = jnp.dot(flat, both_weights, preferred_element_type=jnp.float32).astype(jnp.bfloat16)
    key_value = mixed.reshape(piece.shape[0], piece.shape[1], 2 * columns)
    sequences = queries.shape[0] // SEQ
    seq_rows = queries.reshape(sequences, SEQ, columns)
    shifted = jnp.concatenate(
        [seq_rows[:, SPAN - 1 :], jnp.zeros((sequences, SPAN - 1, columns), jnp.bfloat16)], axis=1
    )
    windows = shifted.reshape(span_count, SPAN * columns)
    want_shard = nbr_shard.reshape(-1)
    want_row = nbr_row.reshape(-1)
    request_count = want_shard.shape[0]
    positions = jnp.arange(request_count, dtype=jnp.int32)
    same_shard = (want_shard[:, None] == want_shard[None, :]) & (
        positions[None, :] < positions[:, None]
    )
    slot_rank = jnp.sum(same_shard.astype(jnp.int32), axis=1)
    slot_index = want_shard * capacity + slot_rank
    onehot_slots = slot_index[:, None] == jnp.arange(slots, dtype=jnp.int32)[None, :]
    send_row = jnp.sum(jnp.where(onehot_slots, want_row[:, None], 0), axis=0).reshape(
        shards, capacity
    )
    selector = jnp.sum(
        onehot_slots.reshape(span_count, neighbours, slots).astype(jnp.bfloat16), axis=1
    )
    send_query = jnp.dot(selector.T, windows, preferred_element_type=jnp.float32).astype(
        jnp.bfloat16
    )
    send_query = send_query.reshape(shards, capacity, SPAN, columns)
    asked = lax.all_to_all(send_query, "db", split_axis=0, concat_axis=0, tiled=True)
    asked_rows = lax.all_to_all(send_row, "db", split_axis=0, concat_axis=0, tiled=True)
    peer_count = asked_rows.shape[0]
    item_count = asked_rows.shape[1]
    group_size = math.gcd(peer_count, 8)
    grouped = asked.reshape(peer_count // group_size, group_size * item_count, SPAN, columns)
    grouped_rows = asked_rows.reshape(peer_count // group_size, group_size * item_count)

    def one_group(operands):
        group_query, group_rows = operands
        picked = jnp.take(key_value, group_rows, axis=0)
        return attend(group_query, picked[..., :columns], picked[..., columns:], DH)

    partial_value, row_max, row_sum = lax.map(one_group, (grouped, grouped_rows))
    partial_value = partial_value.reshape(peer_count, item_count, SPAN, columns)
    row_max = row_max.reshape(peer_count, item_count, head_count, SPAN)
    row_sum = row_sum.reshape(peer_count, item_count, head_count, SPAN)
    partial_value = lax.all_to_all(partial_value, "db", split_axis=0, concat_axis=0, tiled=True)
    row_max, row_sum = (
        lax.all_to_all(row_max, "db", split_axis=0, concat_axis=0, tiled=True),
        lax.all_to_all(row_sum, "db", split_axis=0, concat_axis=0, tiled=True),
    )
    partial_value, row_max, row_sum = (partial_value, row_max, row_sum)
    partial_value = jnp.take(partial_value.reshape(slots, SPAN, columns), slot_index, axis=0)
    row_max = jnp.take(row_max.reshape(slots, head_count, SPAN), slot_index, axis=0)
    row_sum = jnp.take(row_sum.reshape(slots, head_count, SPAN), slot_index, axis=0)
    row_max = row_max.reshape(span_count, neighbours, head_count, SPAN)
    row_sum = row_sum.reshape(span_count, neighbours, head_count, SPAN)
    partial_value = partial_value.reshape(span_count, neighbours, SPAN, head_count, DH).astype(
        jnp.float32
    )
    largest = jnp.max(row_max, axis=1)
    weights_each = jnp.exp(row_max - largest[:, None])
    denominator = jnp.sum(weights_each * row_sum, axis=1)
    numerator = jnp.sum(jnp.swapaxes(weights_each, 2, 3)[..., None] * partial_value, axis=1)
    attended = (numerator / jnp.swapaxes(denominator, 1, 2)[..., None]).astype(jnp.bfloat16)
    attended = attended.reshape(sequences, SEQ, columns)
    result = jnp.concatenate(
        [jnp.zeros((sequences, SPAN - 1, columns), jnp.bfloat16), attended[:, : SEQ - SPAN + 1]],
        axis=1,
    )
    return result.reshape(sequences * SEQ, columns)


def solution(mesh):
    placed = (
        P("db", "mp"),
        P(("db", "mp"), None, None),
        P("db", "mp"),
        P("db", "mp"),
        P("db", None),
        P("db", None),
    )
    return jax.shard_map(
        local, mesh=mesh, in_specs=placed, out_specs=P("db", "mp"), check_vma=False
    )
```

profile of v0, /device:TPU:11, one launch (start us, length us, event | category | flops | bytes accessed | tf_op | source)
XLA Modules:
  0.0 1427.6 jit_solution(8872616640881158538)
XLA Ops:
  28.9 12.5 convolution_convert_fusion
  50.9 175.7 %all-gather.4.cloned.1.call-done = bf16[896,1024]{1,0:T(8,128)(2,1)} async-done(((bf16[56,1024]{1,0:T(8,128)(2,1)}), bf16[896,1024]{1,0:T(8,128)(2,1)}) %all-gather.4.cloned.1.call-update) | async-done | bytes 1835024 | tf_op jit(solution)/shard_map/all_gather | solution.py:46
  226.6 131.3 %all-gather.6.cloned.1.call-done = bf16[896,1024]{1,0:T(8,128)(2,1)} async-done(((bf16[56,1024]{1,0:T(8,128)(2,1)}), bf16[896,1024]{1,0:T(8,128)(2,1)}) %all-gather.6.cloned.1.call-update) | async-done | bytes 1835024 | tf_op jit(solution)/shard_map/all_gather | solution.py:47
  357.9 94.6 %all-gather.8.cloned.1.call-done = bf16[32,128,896]{2,1,0:T(8,128)(2,1)} async-done(((bf16[16,128,896]{2,1,0:T(8,128)(2,1)}), bf16[32,128,896]{2,1,0:T(8,128)(2,1)}) %all-gather.8.cloned.1.call-update) | async-done | bytes 7340048 | tf_op jit(solution)/shard_map/all_gather | solution.py:50
  452.5 24.3 %convert_bitcast_fusion.1 = bf16[4096,2048]{0,1:T(8,128)(2,1)} fusion(bf16[4096,896]{1,0:T(8,128)(2,1)} %bitcast.105, bf16[896,1024]{1,0:T(8,128)(2,1)} %all-gather.6.cloned.1.call-done, bf16[896,1024]{1,0:T(8,128)(2,1)} %all-gather.4.cloned.1.call-done), kind=kOutput, calls=%fused_computation.28 | convolution fusion | flops 15048114176 | bytes 27787264 | tf_op jit(solution)/shard_map/dot_general | solution.py:52
  476.8 22.2 %copy.82 = bf16[4096,2048]{1,0:T(8,128)(2,1)} copy(bf16[4096,2048]{0,1:T(8,128)(2,1)} %convert_bitcast_fusion.1) | data formatting | bytes 33554432 | tf_op jit(solution)/shard_map/while | solution.py:93
  499.0 18.6 %copy.74 = bf16[16,8,64,1024]{3,2,1,0:T(8,128)(2,1)} copy(bf16[16,8,64,1024]{3,1,2,0:T(8,128)(2,1)} %all-to-all-done.1) | data formatting | bytes 33554432 | tf_op jit(solution)/shard_map/all_to_all | solution.py:80
  517.6 460.4 %while.14 = (s32[]{:T(128)}, bf16[2,64,64,1024]{3,2,1,0:T(8,128)(2,1)}, f32[2,64,8,64]{3,2,1,0:T(8,128)S(1)}, f32[2,64,8,64]{3,2,1,0:T(8,128)S(1)}, s32[2,64]{1,...) while((s32[]{:T(128)}, ...), condition=%wide.region_6.7_spmd, body=%wide.region_3.6_spmd.sunk | while | flops 2201945600 | bytes 454563776 | solution.py:93
  538.2 17.9 %gather_fusion = bf16[64,128,2048]{2,1,0:T(8,128)(2,1)} fusion(bf16[32,128,2048]{2,1,0:T(8,128)(2,1)} %get-tuple-element.192, s32[1024]{0:T(1024)S(1)} %pad_clamp_fusion.4), kind=kCustom, calls=%fused_computation.clone.1 | custom fusion | bytes 67109120 | tf_op jit(solution)/shard_map/while/body/eval_jaxpr/jit(_take)/gather | solution.py:90
  556.1 22.8 %broadcast_select_fusion.3 = bf16[64,128,2048]{2,1,0:T(8,128)(2,1)} fusion(bf16[64,128,2048]{2,1,0:T(8,128)(2,1)} %gather_fusion, pred[64]{0:T(512)(128)(4,1)S(1)} %compare_and_fusion.4), kind=kLoop, calls=%fused_computation.4.clone.1 | loop fusion | flops 16777216 | bytes 67108928 | tf_op jit(solution)/shard_map/while/body/eval_jaxpr/jit(_take)/select_n | solution.py:90
  578.9 23.7 %fusion.40 = (bf16[64,128,1024]{2,1,0:T(8,128)(2,1)}, bf16[64,128,1024]{2,1,0:T(8,128)(2,1)}) fusion(bf16[64,128,2048]{2,1,0:T(8,128)(2,1)} %broadcast_select_fusion.3), kind=kLoop, calls=%fused_computation.60.clone.1 | loop fusion | bytes 67108864 | tf_op jit(solution)/shard_map/while/body/eval_jaxpr/slice | solution.py:91
  602.6 22.4 %copy.96 = bf16[64,128,1024]{1,2,0:T(8,128)(2,1)} copy(bf16[64,128,1024]{2,1,0:T(8,128)(2,1)} %get-tuple-element.166) | data formatting | bytes 33554432 | tf_op jit(solution)/shard_map/while/body/eval_jaxpr/slice | solution.py:91
  633.4 8.8 copy.97
  642.3 14.3 %multiply_reduce_fusion.4 = (f32[64,8,64]{2,1,0:T(8,128)S(1)}, f32[64,8,64,128]{3,2,1,0:T(8,128)}) fusion(bf16[64,128,8,128]{1,3,2,0:T(8,128)(2,1)} %bitcast.90, bf16[64,64,8,128]{3,2,1,0:T(8,128)(2,1)} %bitcast.92), kind=kOutput, calls=%fused_computation.6.clone.1 | convolution fusion | flops 1082097664 | bytes 42074112 | tf_op jit(solution)/shard_map/while/body/eval_jaxpr/bqhd,bkhd->bhqk/dot_general | solution.py:18
  656.6 11.0 fusion.41
  667.7 22.4 %copy.95 = bf16[64,128,1024]{1,2,0:T(8,128)(2,1)} copy(bf16[64,128,1024]{2,1,0:T(8,128)(2,1)} %get-tuple-element.165) | data formatting | bytes 33554432 | tf_op jit(solution)/shard_map/while/body/eval_jaxpr/slice | solution.py:91
  690.1 19.0 %convert_bitcast_fusion.3 = bf16[64,64,8,128]{3,1,2,0:T(8,128)(2,1)} fusion(bf16[64,128,8,128]{1,3,2,0:T(8,128)(2,1)} %bitcast.89, f32[64,8,64,128]{3,2,1,0:T(8,128)} %get-tuple-element.167, f32[64,8,64]{2,1,0:T(8,128)S(1)} %get-tuple-element.168), kind=kOutput, calls=%fused_computation.12.clone.1 | convolution fusion | flops 1090519040 | bytes 42074112 | tf_op jit(solution)/shard_map/while/body/eval_jaxpr/bhqk,bkhd->bqhd/dot_general | solution.py:24
  709.1 23.4 %copy.98 = bf16[64,64,8,128]{3,2,1,0:T(8,128)(2,1)} copy(bf16[64,64,8,128]{3,1,2,0:T(8,128)(2,1)} %convert_bitcast_fusion.3) | data formatting | bytes 16777216 | tf_op jit(solution)/shard_map/while/body/eval_jaxpr/convert_element_type | solution.py:31
  732.5 13.3 convert_element_type.72
  754.2 17.9 %gather_fusion = bf16[64,128,2048]{2,1,0:T(8,128)(2,1)} fusion(bf16[32,128,2048]{2,1,0:T(8,128)(2,1)} %get-tuple-element.192, s32[1024]{0:T(1024)S(1)} %pad_clamp_fusion.4), kind=kCustom, calls=%fused_computation.clone.1 | custom fusion | bytes 67109120 | tf_op jit(solution)/shard_map/while/body/eval_jaxpr/jit(_take)/gather | solution.py:90
  772.1 22.8 %broadcast_select_fusion.3 = bf16[64,128,2048]{2,1,0:T(8,128)(2,1)} fusion(bf16[64,128,2048]{2,1,0:T(8,128)(2,1)} %gather_fusion, pred[64]{0:T(512)(128)(4,1)S(1)} %compare_and_fusion.4), kind=kLoop, calls=%fused_computation.4.clone.1 | loop fusion | flops 16777216 | bytes 67108928 | tf_op jit(solution)/shard_map/while/body/eval_jaxpr/jit(_take)/select_n | solution.py:90
  794.9 23.7 %fusion.40 = (bf16[64,128,1024]{2,1,0:T(8,128)(2,1)}, bf16[64,128,1024]{2,1,0:T(8,128)(2,1)}) fusion(bf16[64,128,2048]{2,1,0:T(8,128)(2,1)} %broadcast_select_fusion.3), kind=kLoop, calls=%fused_computation.60.clone.1 | loop fusion | bytes 67108864 | tf_op jit(solution)/shard_map/while/body/eval_jaxpr/slice | solution.py:91
  818.6 22.4 %copy.96 = bf16[64,128,1024]{1,2,0:T(8,128)(2,1)} copy(bf16[64,128,1024]{2,1,0:T(8,128)(2,1)} %get-tuple-element.166) | data formatting | bytes 33554432 | tf_op jit(solution)/shard_map/while/body/eval_jaxpr/slice | solution.py:91
  858.3 14.3 %multiply_reduce_fusion.4 = (f32[64,8,64]{2,1,0:T(8,128)S(1)}, f32[64,8,64,128]{3,2,1,0:T(8,128)}) fusion(bf16[64,128,8,128]{1,3,2,0:T(8,128)(2,1)} %bitcast.90, bf16[64,64,8,128]{3,2,1,0:T(8,128)(2,1)} %bitcast.92), kind=kOutput, calls=%fused_computation.6.clone.1 | convolution fusion | flops 1082097664 | bytes 42074112 | tf_op jit(solution)/shard_map/while/body/eval_jaxpr/bqhd,bkhd->bhqk/dot_general | solution.py:18
  872.6 11.0 fusion.41
  883.7 22.4 %copy.95 = bf16[64,128,1024]{1,2,0:T(8,128)(2,1)} copy(bf16[64,128,1024]{2,1,0:T(8,128)(2,1)} %get-tuple-element.165) | data formatting | bytes 33554432 | tf_op jit(solution)/shard_map/while/body/eval_jaxpr/slice | solution.py:91
  906.1 19.0 %convert_bitcast_fusion.3 = bf16[64,64,8,128]{3,1,2,0:T(8,128)(2,1)} fusion(bf16[64,128,8,128]{1,3,2,0:T(8,128)(2,1)} %bitcast.89, f32[64,8,64,128]{3,2,1,0:T(8,128)} %get-tuple-element.167, f32[64,8,64]{2,1,0:T(8,128)S(1)} %get-tuple-element.168), kind=kOutput, calls=%fused_computation.12.clone.1 | convolution fusion | flops 1090519040 | bytes 42074112 | tf_op jit(solution)/shard_map/while/body/eval_jaxpr/bhqk,bkhd->bqhd/dot_general | solution.py:24
  925.1 23.4 %copy.98 = bf16[64,64,8,128]{3,2,1,0:T(8,128)(2,1)} copy(bf16[64,64,8,128]{3,1,2,0:T(8,128)(2,1)} %convert_bitcast_fusion.3) | data formatting | bytes 16777216 | tf_op jit(solution)/shard_map/while/body/eval_jaxpr/convert_element_type | solution.py:31
  948.5 13.3 convert_element_type.72
  993.3 12.7 all_to_all.29
  1019.6 355.7 %all-to-all-done.3 = bf16[16,8,64,1024]{3,2,1,0:T(8,128)(2,1)} async-done(((bf16[16,8,64,1024]{3,2,1,0:T(8,128)(2,1)}), bf16[16,8,64,1024]{3,2,1,0:T(8,128)(2,1)}, u32[]{:S(2)}, u32[]{:S(2)}) %all-to-all-start.3) | async-done | bytes 16777248 | tf_op jit(solution)/shard_map/all_to_all | solution.py:97
  1375.3 11.3 gather_fusion.1
  (88 shorter events, 137.5 us)
Async XLA Ops:
  7.6 8.8 copy-start.3
  8.2 33.2 %copy-start.5 = (s32[64]{0:T(128)}, s32[64]{0:T(128)S(1)}, u32[]{:S(2)}) copy-start(s32[64]{0:T(128)S(1)} %get-tuple-element.107) | copy-start | bytes 772
  9.8 31.5 %all-to-all-start = ((s32[16,1,8]{2,1,0:T(1,128)}), s32[16,1,8]{2,1,0:T(1,128)S(1)}, u32[]{:S(2)}, u32[]{:S(2)}) async-start(s32[16,1,8]{2,1,0:T(1,128)} %bitcast.8), calls=%async_computation | async-start | bytes 16384 | tf_op jit(solution)/shard_map/all_to_all | solution.py:81
  41.4 457.6 %all-to-all-start.1 = ((bf16[16,8,64,1024]{3,1,2,0:T(8,128)(2,1)}), bf16[16,8,64,1024]{3,1,2,0:T(8,128)(2,1)}, u32[]{:S(2)}, u32[]{:S(2)}) async-start(bf16[16,8,64,1024]{3,1,2,0:T(8,128)(2,1)} %bitcast.95), calls=%async_computation.1 | async-start | bytes 33554432 | tf_op jit(solution)/shard_map/all_to_all | solution.py:80
  47.4 179.2 %all-gather.4.cloned.1.call-start = ((), (), s32[]{:S(2)}) async-start(), calls=%async_computation.5 | async-start | bytes 1949696 | tf_op jit(solution)/shard_map/all_gather | solution.py:46
  48.1 309.8 %all-gather.6.cloned.1.call-start = ((), (), s32[]{:S(2)}) async-start(), calls=%async_computation.6 | async-start | bytes 1949696 | tf_op jit(solution)/shard_map/all_gather | solution.py:47
  48.9 403.6 %all-gather.8.cloned.1.call-start = ((), (), s32[]{:S(2)}) async-start(), calls=%async_computation.7 | async-start | bytes 11010048 | tf_op jit(solution)/shard_map/all_gather | solution.py:50
  979.0 14.3 %all-to-all-start.2 = ((f32[16,1,4096]{2,1,0:T(1,128)}), f32[16,1,4096]{2,1,0:T(1,128)S(1)}, u32[]{:S(2)}, u32[]{:S(2)}) async-start(f32[16,1,4096]{2,1,0:T(1,128)} %reshape.244), calls=%async_computation.2 | async-start | bytes 524288 | tf_op jit(solution)/shard_map/all_to_all | solution.py:99
  1006.0 7.1 copy-start
  1006.0 7.3 copy-start.2
  1006.0 7.4 copy-start.6
  1006.0 7.5 copy-start.4
  1006.0 12.3 copy-start.1
  1006.0 369.2 %all-to-all-start.3 = ((bf16[16,8,64,1024]{3,2,1,0:T(8,128)(2,1)}), bf16[16,8,64,1024]{3,2,1,0:T(8,128)(2,1)}, u32[]{:S(2)}, u32[]{:S(2)}) async-start(bf16[16,8,64,1024]{3,2,1,0:T(8,128)(2,1)} %bitcast.98), calls=%async_computation.3 | async-start | bytes 33554432 | tf_op jit(solution)/shard_map/all_to_all | solution.py:97
Sparse Core Ops, SparseCore 0:
  50.5 176.0 all-gather.3
  228.9 128.9 all-gather.5
  359.5 92.9 all-gather.7
where the time goes:
time: 1440 us; the launch traced here: 1430 us
  waiting for transfers between devices  767 us (53%)
  local copies, waits for them, and re-layouts  390 us (27%)
  matrix products  103 us (7%)
  other arithmetic  86.6 us (6%)
  loops' own time  28.3 us (2%)
  starting transfers between devices  26.5 us (2%)
    all_to_all x1, waiting for transfers between devices, local(): lax.all_to_all(partial_value, 'db', split_axis=0, concat_axis=0, tiled=True)  356 us
    all_gather x1, waiting for transfers between devices, local(): lax.all_gather(key_weight, 'db', axis=0, tiled=True)  176 us
    slice x6, local copies, waits for them, and re-layouts, one_group(): return attend(group_query, picked[..., :columns], picked[..., columns:], DH)  137 us
    all_gather x1, waiting for transfers between devices, local(): lax.all_gather(value_weight, 'db', axis=0, tiled=True)  131 us
    all_gather x1, waiting for transfers between devices, local(): piece = lax.all_gather(encodings, 'mp', axis=0, tiled=True)  94.6 us
    convert_element_type x4, local copies, waits for them, and re-layouts, attend(): partial_value.reshape(batch_size, length, columns).astype(jnp.bfloat16)  73.4 us
    select_n x4, other arithmetic, one_group(): picked = jnp.take(key_value, group_rows, axis=0)  45.6 us
    dot_general x2, matrix products, attend(): jnp.einsum('bhqk,bkhd->bqhd', expscore.astype(jnp.bfloat16), value_heads,...  38 us
  transfers between devices with their start and end apart: 7, of which 5 were waited for; matrix products, arithmetic and copies ran while one was open for 6% of the time, Pallas kernels for 0%

commit v1 on v0

--- a/solution.py
+++ b/solution.py
@@ -7,6 +7,28 @@
 DH = 128
 SPAN = 64
 SEQ = 128
+
+
+def in_order(pieces, dim):
+    pieces = jnp.moveaxis(pieces, 0, dim)
+    lengths = pieces.shape
+    return pieces.reshape(*lengths[:dim], lengths[dim] * lengths[dim + 1], *lengths[dim + 2 :])
+
+
+def gather_around(x, axis, dim):
+    count = lax.axis_size(axis)
+    pairs = [(i, (i + 1) % count) for i in range(count)]
+    back = [(b, a) for a, b in pairs]
+    lower, upper = ([], [])
+    for step in range(count - 1):
+        if step % 2 == 0:
+            lower.append(lax.ppermute(lower[-1] if lower else x, axis, pairs))
+        else:
+            upper.append(lax.ppermute(upper[-1] if upper else x, axis, back))
+    pieces = jnp.stack([*lower[::-1], x, *upper])
+    shift = lax.axis_index(axis) - len(lower)
+    pieces = pieces[(jnp.arange(count) - shift) % count]
+    return in_order(pieces, dim)
 
 
 def attend(queried, key_block, value_block, head_dim):
@@ -44,7 +66,7 @@
     slots = shards * capacity
     full_keys, full_values = (
         lax.all_gather(key_weight, "db", axis=0, tiled=True),
-        lax.all_gather(value_weight, "db", axis=0, tiled=True),
+        gather_around(value_weight, "db", 0),
     )
     both_weights = jnp.concatenate([full_keys, full_values], axis=1)
     piece = lax.all_gather(encodings, "mp", axis=0, tiled=True)

time: 1440 us -> 1460 us (1.014)
  starting transfers between devices: 26.5 us -> 52.1 us
  waiting for transfers between devices: 767 us -> 744 us
    ppermute x0 -> x15, waiting for transfers between devices: none -> 380 us  [the longest x8 380 us: gather_around(): lower.append(lax.ppermute(lower[-1] if lower else x, axis, pairs))]
    all_gather x1, waiting for transfers between devices: 176 us -> 0.01 us  [local(): lax.all_gather(key_weight, 'db', axis=0, tiled=True)]
    all_gather x1 -> x0, waiting for transfers between devices: 131 us -> none  [local(): lax.all_gather(value_weight, 'db', axis=0, tiled=True)]
    all_gather x1, waiting for transfers between devices: 94.6 us -> 0.01 us  [local(): piece = lax.all_gather(encodings, 'mp', axis=0, tiled=True)]
    ppermute x0 -> x15, starting transfers between devices: none -> 25.5 us  [the longest x8 25 us: gather_around(): lower.append(lax.ppermute(lower[-1] if lower else x, axis, pairs))]
  transfers between devices with their start and end apart: 7 -> 21, of which waited for: 5 -> 10; matrix products, arithmetic and copies ran while one was open for 6% -> 6% of each run, Pallas kernels for 0% -> 0%
where the time goes in v1:
time: 1460 us; the launch traced here: 1440 us
  waiting for transfers between devices  744 us (51%)
  local copies, waits for them, and re-layouts  402 us (28%)
  matrix products  104 us (7%)
  other arithmetic  86.4 us (6%)
  starting transfers between devices  52.1 us (4%)
  loops' own time  28.3 us (2%)
    ppermute x8, waiting for transfers between devices, gather_around(): lower.append(lax.ppermute(lower[-1] if lower else x, axis, pairs))  380 us
    all_to_all x1, waiting for transfers between devices, local(): lax.all_to_all(partial_value, 'db', split_axis=0, concat_axis=0, tiled=True)  356 us
    slice x6, local copies, waits for them, and re-layouts, one_group(): return attend(group_query, picked[..., :columns], picked[..., columns:], DH)  137 us
    convert_element_type x4, local copies, waits for them, and re-layouts, attend(): partial_value.reshape(batch_size, length, columns).astype(jnp.bfloat16)  73.5 us
    select_n x4, other arithmetic, one_group(): picked = jnp.take(key_value, group_rows, axis=0)  45.6 us
    dot_general x2, matrix products, attend(): jnp.einsum('bhqk,bkhd->bqhd', expscore.astype(jnp.bfloat16), value_heads,...  38.1 us
    gather x2, local copies, waits for them, and re-layouts, one_group(): picked = jnp.take(key_value, group_rows, axis=0)  35.8 us
  transfers between devices with their start and end apart: 21, of which 10 were waited for; matrix products, arithmetic and copies ran while one was open for 6% of the time, Pallas kernels for 0%

profile of v1, /device:TPU:11, one launch (start us, length us, event | category | flops | bytes accessed | tf_op | source)
XLA Modules:
  0.0 1443.7 jit_solution(8500112173501881233)
XLA Ops:
  28.8 12.5 convolution_convert_fusion
  50.5 369.6 %collective-permute-done = bf16[56,1024]{1,0:T(8,128)(2,1)S(1)} collective-permute-done((bf16[56,1024]{1,0:T(8,128)(2,1)S(1)}, bf16[56,1024]{1,0:T(8,128)(2,1)S(1)}, u32[]{:S(2)}, u32[]{:S(2)}) %collective-permute-start) | collective-permute-done | bytes 114720 | tf_op jit(solution)/shard_map/ppermute | solution.py:25
  467.2 24.3 %convert_bitcast_fusion.1 = bf16[4096,2048]{0,1:T(8,128)(2,1)} fusion(bf16[4096,896]{1,0:T(8,128)(2,1)} %bitcast.141, bf16[896,1024]{1,0:T(8,128)(2,1)} %bitcast.134, bf16[896,1024]{1,0:T(8,128)(2,1)} %all-gather.3.cloned.1.call-done), kind=kOutput, calls=%fused_computation.29 | convolution fusion | flops 15048114176 | bytes 27787264 | tf_op jit(solution)/shard_map/dot_general | solution.py:74
  491.5 22.6 %copy.82 = bf16[4096,2048]{1,0:T(8,128)(2,1)} copy(bf16[4096,2048]{0,1:T(8,128)(2,1)} %convert_bitcast_fusion.1) | data formatting | bytes 33554432 | tf_op jit(solution)/shard_map/while | solution.py:115
  514.1 18.6 %copy.74 = bf16[16,8,64,1024]{3,2,1,0:T(8,128)(2,1)} copy(bf16[16,8,64,1024]{3,1,2,0:T(8,128)(2,1)} %all-to-all-done.1) | data formatting | bytes 33554432 | tf_op jit(solution)/shard_map/all_to_all | solution.py:102
  532.8 460.8 %while.14 = (s32[]{:T(128)}, bf16[2,64,64,1024]{3,2,1,0:T(8,128)(2,1)}, f32[2,64,8,64]{3,2,1,0:T(8,128)S(1)}, f32[2,64,8,64]{3,2,1,0:T(8,128)S(1)}, s32[2,64]{1,...) while((s32[]{:T(128)}, ...), condition=%wide.region_6.7_spmd, body=%wide.region_3.6_spmd.sunk | while | flops 2201945600 | bytes 454563776 | solution.py:115
  553.3 17.9 %gather_fusion = bf16[64,128,2048]{2,1,0:T(8,128)(2,1)} fusion(bf16[32,128,2048]{2,1,0:T(8,128)(2,1)} %get-tuple-element.192, s32[1024]{0:T(1024)S(1)} %pad_clamp_fusion.5), kind=kCustom, calls=%fused_computation.clone.1 | custom fusion | bytes 67109120 | tf_op jit(solution)/shard_map/while/body/eval_jaxpr/jit(_take)/gather | solution.py:112
  571.3 22.8 %broadcast_select_fusion.3 = bf16[64,128,2048]{2,1,0:T(8,128)(2,1)} fusion(bf16[64,128,2048]{2,1,0:T(8,128)(2,1)} %gather_fusion, pred[64]{0:T(512)(128)(4,1)S(1)} %compare_and_fusion.4), kind=kLoop, calls=%fused_computation.5.clone.1 | loop fusion | flops 16777216 | bytes 67108928 | tf_op jit(solution)/shard_map/while/body/eval_jaxpr/jit(_take)/select_n | solution.py:112
  594.1 23.8 %fusion.42 = (bf16[64,128,1024]{2,1,0:T(8,128)(2,1)}, bf16[64,128,1024]{2,1,0:T(8,128)(2,1)}) fusion(bf16[64,128,2048]{2,1,0:T(8,128)(2,1)} %broadcast_select_fusion.3), kind=kLoop, calls=%fused_computation.84.clone.1 | loop fusion | bytes 67108864 | tf_op jit(solution)/shard_map/while/body/eval_jaxpr/slice | solution.py:113
  617.8 22.3 %copy.96 = bf16[64,128,1024]{1,2,0:T(8,128)(2,1)} copy(bf16[64,128,1024]{2,1,0:T(8,128)(2,1)} %get-tuple-element.166) | data formatting | bytes 33554432 | tf_op jit(solution)/shard_map/while/body/eval_jaxpr/slice | solution.py:113
  648.6 8.9 copy.97
  657.5 14.4 multiply_reduce_fusion.4
  671.8 11.0 fusion.43
  682.9 22.4 %copy.95 = bf16[64,128,1024]{1,2,0:T(8,128)(2,1)} copy(bf16[64,128,1024]{2,1,0:T(8,128)(2,1)} %get-tuple-element.165) | data formatting | bytes 33554432 | tf_op jit(solution)/shard_map/while/body/eval_jaxpr/slice | solution.py:113
  705.3 19.1 %convert_bitcast_fusion.3 = bf16[64,64,8,128]{3,1,2,0:T(8,128)(2,1)} fusion(bf16[64,128,8,128]{1,3,2,0:T(8,128)(2,1)} %bitcast.124, f32[64,8,64,128]{3,2,1,0:T(8,128)} %get-tuple-element.167, f32[64,8,64]{2,1,0:T(8,128)S(1)} %get-tuple-element.168), kind=kOutput, calls=%fused_computation.13.clone.1 | convolution fusion | flops 1090519040 | bytes 42074112 | tf_op jit(solution)/shard_map/while/body/eval_jaxpr/bhqk,bkhd->bqhd/dot_general | solution.py:46
  724.4 23.4 %copy.98 = bf16[64,64,8,128]{3,2,1,0:T(8,128)(2,1)} copy(bf16[64,64,8,128]{3,1,2,0:T(8,128)(2,1)} %convert_bitcast_fusion.3) | data formatting | bytes 16777216 | tf_op jit(solution)/shard_map/while/body/eval_jaxpr/convert_element_type | solution.py:53
  747.8 13.3 convert_element_type.72
  769.5 17.9 %gather_fusion = bf16[64,128,2048]{2,1,0:T(8,128)(2,1)} fusion(bf16[32,128,2048]{2,1,0:T(8,128)(2,1)} %get-tuple-element.192, s32[1024]{0:T(1024)S(1)} %pad_clamp_fusion.5), kind=kCustom, calls=%fused_computation.clone.1 | custom fusion | bytes 67109120 | tf_op jit(solution)/shard_map/while/body/eval_jaxpr/jit(_take)/gather | solution.py:112
  787.5 22.8 %broadcast_select_fusion.3 = bf16[64,128,2048]{2,1,0:T(8,128)(2,1)} fusion(bf16[64,128,2048]{2,1,0:T(8,128)(2,1)} %gather_fusion, pred[64]{0:T(512)(128)(4,1)S(1)} %compare_and_fusion.4), kind=kLoop, calls=%fused_computation.5.clone.1 | loop fusion | flops 16777216 | bytes 67108928 | tf_op jit(solution)/shard_map/while/body/eval_jaxpr/jit(_take)/select_n | solution.py:112
  810.3 23.8 %fusion.42 = (bf16[64,128,1024]{2,1,0:T(8,128)(2,1)}, bf16[64,128,1024]{2,1,0:T(8,128)(2,1)}) fusion(bf16[64,128,2048]{2,1,0:T(8,128)(2,1)} %broadcast_select_fusion.3), kind=kLoop, calls=%fused_computation.84.clone.1 | loop fusion | bytes 67108864 | tf_op jit(solution)/shard_map/while/body/eval_jaxpr/slice | solution.py:113
  834.0 22.3 %copy.96 = bf16[64,128,1024]{1,2,0:T(8,128)(2,1)} copy(bf16[64,128,1024]{2,1,0:T(8,128)(2,1)} %get-tuple-element.166) | data formatting | bytes 33554432 | tf_op jit(solution)/shard_map/while/body/eval_jaxpr/slice | solution.py:113
  864.8 8.9 copy.97
  873.7 14.4 multiply_reduce_fusion.4
  888.0 11.0 fusion.43
  899.1 22.4 %copy.95 = bf16[64,128,1024]{1,2,0:T(8,128)(2,1)} copy(bf16[64,128,1024]{2,1,0:T(8,128)(2,1)} %get-tuple-element.165) | data formatting | bytes 33554432 | tf_op jit(solution)/shard_map/while/body/eval_jaxpr/slice | solution.py:113
  921.5 19.1 %convert_bitcast_fusion.3 = bf16[64,64,8,128]{3,1,2,0:T(8,128)(2,1)} fusion(bf16[64,128,8,128]{1,3,2,0:T(8,128)(2,1)} %bitcast.124, f32[64,8,64,128]{3,2,1,0:T(8,128)} %get-tuple-element.167, f32[64,8,64]{2,1,0:T(8,128)S(1)} %get-tuple-element.168), kind=kOutput, calls=%fused_computation.13.clone.1 | convolution fusion | flops 1090519040 | bytes 42074112 | tf_op jit(solution)/shard_map/while/body/eval_jaxpr/bhqk,bkhd->bqhd/dot_general | solution.py:46
  940.6 23.4 %copy.98 = bf16[64,64,8,128]{3,2,1,0:T(8,128)(2,1)} copy(bf16[64,64,8,128]{3,1,2,0:T(8,128)(2,1)} %convert_bitcast_fusion.3) | data formatting | bytes 16777216 | tf_op jit(solution)/shard_map/while/body/eval_jaxpr/convert_element_type | solution.py:53
  964.0 13.3 convert_element_type.72
  1009.2 12.7 all_to_all.29
  1035.4 355.7 %all-to-all-done.3 = bf16[16,8,64,1024]{3,2,1,0:T(8,128)(2,1)} async-done(((bf16[16,8,64,1024]{3,2,1,0:T(8,128)(2,1)}), bf16[16,8,64,1024]{3,2,1,0:T(8,128)(2,1)}, u32[]{:S(2)}, u32[]{:S(2)}) %all-to-all-start.3) | async-done | bytes 16777248 | tf_op jit(solution)/shard_map/all_to_all | solution.py:119
  1391.1 11.3 gather_fusion.2
  1411.2 8.8 multiply_reduce_fusion.1
  (152 shorter events, 166.8 us)
Async XLA Ops:
  7.6 8.7 copy-start.12
  8.1 20.7 %copy-start.14 = (s32[64]{0:T(128)}, s32[64]{0:T(128)S(1)}, u32[]{:S(2)}) copy-start(s32[64]{0:T(128)S(1)} %get-tuple-element.107) | copy-start | bytes 772
  9.8 31.5 %all-to-all-start = ((s32[16,1,8]{2,1,0:T(1,128)}), s32[16,1,8]{2,1,0:T(1,128)S(1)}, u32[]{:S(2)}, u32[]{:S(2)}) async-start(s32[16,1,8]{2,1,0:T(1,128)} %bitcast.8), calls=%async_computation | async-start | bytes 16384 | tf_op jit(solution)/shard_map/all_to_all | solution.py:103
  41.3 7.6 copy-start
  41.3 472.8 %all-to-all-start.1 = ((bf16[16,8,64,1024]{3,1,2,0:T(8,128)(2,1)}), bf16[16,8,64,1024]{3,1,2,0:T(8,128)(2,1)}, u32[]{:S(2)}, u32[]{:S(2)}) async-start(bf16[16,8,64,1024]{3,1,2,0:T(8,128)(2,1)} %bitcast.130), calls=%async_computation.1 | async-start | bytes 33554432 | tf_op jit(solution)/shard_map/all_to_all | solution.py:102
  47.4 419.8 %all-gather.3.cloned.1.call-start = ((), (), s32[]{:S(2)}) async-start(), calls=%async_computation.5 | async-start | bytes 1949696 | tf_op jit(solution)/shard_map/all_gather | solution.py:68
  48.2 419.0 %all-gather.5.cloned.1.call-start = ((), (), s32[]{:S(2)}) async-start(), calls=%async_computation.6 | async-start | bytes 11010048 | tf_op jit(solution)/shard_map/all_gather | solution.py:72
  48.9 371.1 %collective-permute-start = (bf16[56,1024]{1,0:T(8,128)(2,1)S(1)}, bf16[56,1024]{1,0:T(8,128)(2,1)S(1)}, u32[]{:S(2)}, u32[]{:S(2)}) collective-permute-start(bf16[56,1024]{1,0:T(8,128)(2,1)S(1)} %copy-done), channel_id=1, source_target_pairs={{0,2},{2,4},{4,6},{6,8},{8,10},{10,12},{12,14},{14,16},{16,18},{18... | collective-permute-start | bytes 344072 | tf_op jit(solution)/shard_map/ppermute | solution.py:25
  420.0 5.2 collective-permute-start.1
  423.4 5.2 collective-permute-start.8
  425.2 5.2 collective-permute-start.2
  428.6 5.2 collective-permute-start.9
  430.4 8.5 copy-start.1
  430.4 5.2 collective-permute-start.3
  433.7 5.2 collective-permute-start.10
  435.5 20.4 %copy-start.4 = (bf16[56,1024]{1,0:T(8,128)(2,1)}, bf16[56,1024]{1,0:T(8,128)(2,1)S(1)}, u32[]{:S(2)}) copy-start(bf16[56,1024]{1,0:T(8,128)(2,1)S(1)} %collective-permute-done.3) | copy-start | bytes 344068
  435.5 5.2 collective-permute-start.4
  438.9 5.2 collective-permute-start.11
  440.7 15.3 %copy-start.6 = (bf16[56,1024]{1,0:T(8,128)(2,1)}, bf16[56,1024]{1,0:T(8,128)(2,1)S(1)}, u32[]{:S(2)}) copy-start(bf16[56,1024]{1,0:T(8,128)(2,1)S(1)} %collective-permute-done.4) | copy-start | bytes 344068
  440.7 5.2 collective-permute-start.5
  444.1 11.9 copy-start.3
  444.1 5.1 collective-permute-start.12
  445.8 10.2 copy-start.7
  445.9 5.2 collective-permute-start.6
  449.2 6.3 collective-permute-start.13
  451.0 5.1 collective-permute-start.7
  455.5 9.7 collective-permute-start.14
  994.5 14.6 %all-to-all-start.2 = ((f32[16,1,4096]{2,1,0:T(1,128)}), f32[16,1,4096]{2,1,0:T(1,128)S(1)}, u32[]{:S(2)}, u32[]{:S(2)}) async-start(f32[16,1,4096]{2,1,0:T(1,128)} %reshape.305), calls=%async_computation.2 | async-start | bytes 524288 | tf_op jit(solution)/shard_map/all_to_all | solution.py:121
  1021.9 7.4 copy-start.15
  1021.9 7.4 copy-start.13
  1021.9 12.3 copy-start.10
  1021.9 369.2 %all-to-all-start.3 = ((bf16[16,8,64,1024]{3,2,1,0:T(8,128)(2,1)}), bf16[16,8,64,1024]{3,2,1,0:T(8,128)(2,1)}, u32[]{:S(2)}, u32[]{:S(2)}) async-start(bf16[16,8,64,1024]{3,2,1,0:T(8,128)(2,1)} %bitcast.133), calls=%async_computation.3 | async-start | bytes 33554432 | tf_op jit(solution)/shard_map/all_to_all | solution.py:119
  (5 other events, 26.9 us)
Sparse Core Ops, SparseCore 0:
  50.5 176.0 all-gather.2
  228.2 151.6 all-gather.4
